TPU v7x, 128 devices: a whole 4x4x4 slice. The times are simulated.
128 devices in a mesh: samp: 32 (over y, z, core), layer: 4 (over x).
Axes of the slice: x: 4, y: 4, z: 4, core: 2. Of those that a mesh axis runs over, the one named last changes fastest.
Arguments:
- spins: int32 [256, 256], P('samp'), may hold values 0 or 1
- activations: bfloat16 [256, 8, 256, 256], P('samp', 'layer'), may hold values from -6 to 6
- cotangents: bfloat16 [256, 8, 256, 256], P('samp', 'layer'), may hold values from -0.023925781 to 0.023925781
- offdiag: float32 [256], P('samp'), may hold values from -24 to 24
Outputs:
- weights: float32 [256], P('samp')
- update: float32 [8, 256, 256], P('layer', 'samp')
All inputs are finite; a program needn't handle non-finite values. No bound on the sum of `spins` on one device may be relied on, other than what follows from the above.
Results may differ from a plain program's by a relative error of at most 0.0029.
Values may be sent and summed in bfloat16 or wider, within the bound.
A program may use at most 64 MiB of HBM per device.

v0:
```python
import jax
import jax.numpy as jnp
from jax import lax
from jax.sharding import PartitionSpec as P

SIDE = 16
shift_ratio = 0.1
highest = lax.Precision.HIGHEST


def laid_out(parts, dim):
    parts = jnp.moveaxis(parts, 0, dim)
    dims = parts.shape
    return parts.reshape(*dims[:dim], dims[dim] * dims[dim + 1], *dims[dim + 2 :])


def copy_for_each(shard, axis):
    length = lax.axis_size(axis)
    return lax.all_to_all(
        jnp.broadcast_to(shard[None], (length, *shard.shape)), axis, 0, 0, tiled=True
    )


def gather_directly(shard, axis, dim):
    return laid_out(copy_for_each(shard, axis), dim)


def local_energy(spins, offdiag):
    zvals = (2 * spins - 1).astype(jnp.float32).reshape(spins.shape[0], SIDE, SIDE)
    bonds = zvals * jnp.roll(zvals, -1, 2) + zvals * jnp.roll(zvals, -1, 1)
    return offdiag + jnp.sum(bonds, axis=(1, 2))


def small_factor(matrix):
    order = matrix.shape[0]
    positions = lax.iota(jnp.int32, order)

    def one_column(j, carry):
        rest, lower = carry
        column = lax.dynamic_slice_in_dim(rest, j, 1, 1)[:, 0]
        pivot = jnp.sqrt(lax.dynamic_slice_in_dim(column, j, 1)[0])
        scaled = jnp.where(positions >= j, column / pivot, jnp.float32(0.0))
        lower = lax.dynamic_update_slice_in_dim(lower, scaled[:, None], j, 1)
        rest = rest - scaled[:, None] * scaled[None, :]
        return (rest, lower)

    start = (matrix, jnp.zeros_like(matrix))
    return lax.fori_loop(0, order, one_column, start)[1]


def lower_inverse(lower):
    order = lower.shape[0]
    ident = jnp.eye(order, dtype=jnp.float32)

    def one_row(i, inverse):
        lower_row = lax.dynamic_slice_in_dim(lower, i, 1, 0)
        unit_row = lax.dynamic_slice_in_dim(ident, i, 1, 0)
        diag_entry = lax.dynamic_slice_in_dim(lower_row[0], i, 1)[0]
        known = jnp.dot(lower_row, inverse, precision=highest)
        fresh = (unit_row - known) / diag_entry
        return lax.dynamic_update_slice_in_dim(inverse, fresh, i, 0)

    return lax.fori_loop(0, order, one_row, jnp.zeros_like(lower))


def blocked_solve(matrix, rhs):
    block = matrix.shape[0] // 8
    lower_tiles = {}
    inverses = []
    for k in range(8):
        diag_tile = matrix[k * block : (k + 1) * block, k * block : (k + 1) * block]
        for c in range(k):
            diag_tile = diag_tile - jnp.dot(
                lower_tiles[k, c], lower_tiles[k, c].T, precision=highest
            )
        factor = small_factor(diag_tile)
        inverse = lower_inverse(factor)
        inverses.append(inverse)
        for r in range(k + 1, 8):
            tile = matrix[r * block : (r + 1) * block, k * block : (k + 1) * block]
            for c in range(k):
                tile = tile - jnp.dot(lower_tiles[r, c], lower_tiles[k, c].T, precision=highest)
            lower_tiles[r, k] = jnp.dot(tile, inverse.T, precision=highest)
    forward = []
    for k in range(8):
        piece = rhs[k * block : (k + 1) * block]
        for c in range(k):
            piece = piece - jnp.dot(lower_tiles[k, c], forward[c], precision=highest)
        forward.append(jnp.dot(inverses[k], piece, precision=highest))
    backward = [None] * 8
    for k in range(7, -1, -1):
        piece = forward[k]
        for r in range(k + 1, 8):
            piece = piece - jnp.dot(lower_tiles[r, k].T, backward[r], precision=highest)
        backward[k] = jnp.dot(inverses[k].T, piece, precision=highest)
    return jnp.concatenate(backward)


def body(spins, activations, cotangents, offdiag):
    s_local = spins.shape[0]
    energy_local = local_energy(spins, offdiag)
    energy = gather_directly(energy_local, "samp", 0)
    total = energy.shape[0]
    eps = (energy - jnp.mean(energy)) / jnp.sqrt(jnp.float32(total))
    jac = jnp.einsum(
        "ksad,ksae->ksde", activations, cotangents, preferred_element_type=jnp.float32
    ).astype(jnp.bfloat16)
    regrouped = lax.all_to_all(jac, "samp", split_axis=2, concat_axis=0, tiled=True)
    flat = regrouped.reshape(total, -1)
    col_mean = jnp.mean(flat, axis=0, dtype=jnp.float32)
    raw_gram = jnp.dot(flat, flat.T, preferred_element_type=jnp.float32)
    row_dots = jnp.dot(flat.astype(jnp.float32), col_mean, precision=highest)
    mean_square = jnp.sum(col_mean * col_mean)
    partial_value = (raw_gram - row_dots[:, None] - row_dots[None, :] + mean_square) / total
    gram = lax.psum(partial_value, ("samp", "layer"))
    shift = shift_ratio * jnp.trace(gram) / total
    weights = blocked_solve(gram + shift * jnp.eye(total, dtype=jnp.float32), eps)
    start = lax.axis_index("samp") * s_local
    own_weights = lax.dynamic_slice_in_dim(weights, start, s_local)
    coeffs_all = weights - jnp.mean(weights)
    update = jnp.dot(coeffs_all, flat.astype(jnp.float32), precision=highest).reshape(
        regrouped.shape[1:]
    )
    return (own_weights, update)


def solution(mesh):
    placed = (
        P("samp", None),
        P("samp", "layer", None, None),
        P("samp", "layer", None, None),
        P("samp"),
    )
    return jax.shard_map(
        body,
        mesh=mesh,
        in_specs=placed,
        out_specs=(P("samp"), P("layer", "samp", None)),
        check_vma=False,
    )
```

profile of v0, /device:TPU:1, one launch (start us, length us, event | category | flops | bytes accessed | tf_op | source)
XLA Modules:
  0.0 995.8 jit_solution(18253489442866644126)
XLA Ops:
  7.2 0.9 add_convert_fusion
  8.4 0.8 multiply_reduce_fusion.1
  10.5 9.6 all-to-all-start.1
  20.1 2.4 convolution_convert_fusion
  22.5 3.5 copy.85
  25.9 1.0 all-to-all-done.1
  27.0 6.4 all-to-all-start
  34.7 27.0 %all-to-all-done = bf16[8,2,256,256]{3,1,0,2:T(2,128)(2,1)} async-done(((bf16[8,2,256,256]{3,1,0,2:T(2,128)(2,1)}), bf16[8,2,256,256]{3,1,0,2:T(2,128)(2,1)}, u32[]{:S(2)}, u32[]{:S(2)}) %all-to-all-start) | async-done | bytes 2097184 | tf_op jit(solution)/shard_map/all_to_all | solution.py:108
  61.7 2.8 convert_reduce_fusion
  64.5 4.2 copy.135
  68.8 4.2 reshape.493
  73.6 3.5 fusion.238
  77.1 2.1 fusion.52
  79.9 3.6 copy.128
  83.5 134.9 %all-reduce.2.cloned.1.call-done = f32[256,256]{1,0:T(8,128)} async-done(((f32[256,256]{1,0:T(8,128)}), f32[256,256]{1,0:T(8,128)}) %all-reduce.2.cloned.1.call-update) | async-done | bytes 262160 | tf_op jit(solution)/shard_map/psum | solution.py:115
  218.4 1.6 select_reduce_fusion
  220.6 1.0 select_add_fusion
  221.7 44.8 %while.288 = (s32[]{:T(128)}, f32[32,32]{0,1:T(8,128)S(1)}, f32[32,32]{0,1:T(8,128)S(1)}, s32[]{:T(128)}, s32[]{:T(128)}, /*index=5*/s32[]{:T(128)}) while((s32[]{:T(128)}, f32[32,32]{0,1:T(8,128)S(1)}, f32[32,32]{0,1:T(8,128)S(1)}, s32[]{:T(128)}, s32[]{:T(128)}, /*index=5*/s32[]{:T(128)}) %tuple.681), condition=%wide.region_5.6_spmd.clone, body=%wide.region_4.5_spmd.clone.sunk | while | flops 2211 | bytes 10493 | solution.py:48
  266.6 45.1 %while.280 = (s32[]{:T(128)}, f32[32,32]{1,0:T(8,128)S(1)}, f32[32,32]{1,0:T(8,128)S(1)}, f32[32,32]{1,0:T(8,128)S(1)}, s32[]{:T(128)}, /*index=5*/s32[]{:T(128)}, s32[]{:T(128)}) while((s32[]{:T(128)}, f32[32,32]{1,0:T(8,128)S(1)}, f32[32,32]{1,0:T(8,128)S(1)}, f32[32,32]{1,0:T(8,128)S(1)}, s32[]{:T(128)}, /*index=5*/s32[]{:T(128)}, ...), condition=%wide.region_7.8_spmd, body=%wide.region_6.7_spmd.sunk | while | flops 12355 | bytes 18937 | solution.py:63
  268.6 0.8 fusion.577
  270.0 0.8 fusion.577
  272.8 0.8 fusion.577
  274.2 0.8 fusion.577
  277.0 0.8 fusion.577
  279.9 0.8 fusion.577
  281.3 0.8 fusion.577
  284.1 0.8 fusion.577
  285.5 0.8 fusion.577
  288.3 0.8 fusion.577
  289.7 0.8 fusion.577
  291.1 0.8 fusion.577
  292.5 0.8 fusion.577
  318.4 45.6 %while.289 = (s32[]{:T(128)}, f32[32,32]{0,1:T(8,128)S(1)}, f32[32,32]{0,1:T(8,128)S(1)}, s32[]{:T(128)}, s32[]{:T(128)}, /*index=5*/s32[]{:T(128)}) while((s32[]{:T(128)}, f32[32,32]{0,1:T(8,128)S(1)}, f32[32,32]{0,1:T(8,128)S(1)}, s32[]{:T(128)}, s32[]{:T(128)}, /*index=5*/s32[]{:T(128)}) %tuple.687), condition=%wide.region_11.12_spmd.clone, body=%wide.region_10.11_spmd.clone.sunk | while | flops 2211 | bytes 10493 | solution.py:48
  364.0 45.1 %while.281 = (s32[]{:T(128)}, f32[32,32]{1,0:T(8,128)S(1)}, f32[32,32]{1,0:T(8,128)S(1)}, f32[32,32]{1,0:T(8,128)S(1)}, s32[]{:T(128)}, /*index=5*/s32[]{:T(128)}, s32[]{:T(128)}) while((s32[]{:T(128)}, f32[32,32]{1,0:T(8,128)S(1)}, f32[32,32]{1,0:T(8,128)S(1)}, f32[32,32]{1,0:T(8,128)S(1)}, s32[]{:T(128)}, /*index=5*/s32[]{:T(128)}, ...), condition=%wide.region_13.14_spmd, body=%wide.region_12.13_spmd.sunk | while | flops 12355 | bytes 18937 | solution.py:63
  412.9 45.5 %while.290 = (s32[]{:T(128)}, f32[32,32]{0,1:T(8,128)S(1)}, f32[32,32]{0,1:T(8,128)S(1)}, s32[]{:T(128)}, s32[]{:T(128)}, /*index=5*/s32[]{:T(128)}) while((s32[]{:T(128)}, f32[32,32]{0,1:T(8,128)S(1)}, f32[32,32]{0,1:T(8,128)S(1)}, s32[]{:T(128)}, s32[]{:T(128)}, /*index=5*/s32[]{:T(128)}) %tuple.693), condition=%wide.region_15.16_spmd.clone, body=%wide.region_14.15_spmd.clone.sunk | while | flops 2211 | bytes 10493 | solution.py:48
  458.5 45.1 %while.282 = (s32[]{:T(128)}, f32[32,32]{1,0:T(8,128)S(1)}, f32[32,32]{1,0:T(8,128)S(1)}, f32[32,32]{1,0:T(8,128)S(1)}, s32[]{:T(128)}, /*index=5*/s32[]{:T(128)}, s32[]{:T(128)}) while((s32[]{:T(128)}, f32[32,32]{1,0:T(8,128)S(1)}, f32[32,32]{1,0:T(8,128)S(1)}, f32[32,32]{1,0:T(8,128)S(1)}, s32[]{:T(128)}, /*index=5*/s32[]{:T(128)}, ...), condition=%wide.region_17.18_spmd, body=%wide.region_16.17_spmd.sunk | while | flops 12355 | bytes 18937 | solution.py:63
  507.4 45.5 %while.291 = (s32[]{:T(128)}, f32[32,32]{0,1:T(8,128)S(1)}, f32[32,32]{0,1:T(8,128)S(1)}, s32[]{:T(128)}, s32[]{:T(128)}, /*index=5*/s32[]{:T(128)}) while((s32[]{:T(128)}, f32[32,32]{0,1:T(8,128)S(1)}, f32[32,32]{0,1:T(8,128)S(1)}, s32[]{:T(128)}, s32[]{:T(128)}, /*index=5*/s32[]{:T(128)}) %tuple.699), condition=%wide.region_19.20_spmd.clone, body=%wide.region_18.19_spmd.clone.sunk | while | flops 2211 | bytes 10493 | solution.py:48
  553.0 45.1 %while.283 = (s32[]{:T(128)}, f32[32,32]{1,0:T(8,128)S(1)}, f32[32,32]{1,0:T(8,128)S(1)}, f32[32,32]{1,0:T(8,128)S(1)}, s32[]{:T(128)}, /*index=5*/s32[]{:T(128)}, s32[]{:T(128)}) while((s32[]{:T(128)}, f32[32,32]{1,0:T(8,128)S(1)}, f32[32,32]{1,0:T(8,128)S(1)}, f32[32,32]{1,0:T(8,128)S(1)}, s32[]{:T(128)}, /*index=5*/s32[]{:T(128)}, ...), condition=%wide.region_21.22_spmd, body=%wide.region_20.21_spmd.sunk | while | flops 12355 | bytes 18937 | solution.py:63
  601.6 45.5 %while.292 = (s32[]{:T(128)}, f32[32,32]{0,1:T(8,128)S(1)}, f32[32,32]{0,1:T(8,128)S(1)}, s32[]{:T(128)}, s32[]{:T(128)}, /*index=5*/s32[]{:T(128)}) while((s32[]{:T(128)}, f32[32,32]{0,1:T(8,128)S(1)}, f32[32,32]{0,1:T(8,128)S(1)}, s32[]{:T(128)}, s32[]{:T(128)}, /*index=5*/s32[]{:T(128)}) %tuple.705), condition=%wide.region_23.24_spmd.clone, body=%wide.region_22.23_spmd.clone.sunk | while | flops 2211 | bytes 10493 | solution.py:48
  647.2 45.1 %while.284 = (s32[]{:T(128)}, f32[32,32]{1,0:T(8,128)S(1)}, f32[32,32]{1,0:T(8,128)S(1)}, f32[32,32]{1,0:T(8,128)S(1)}, s32[]{:T(128)}, /*index=5*/s32[]{:T(128)}, s32[]{:T(128)}) while((s32[]{:T(128)}, f32[32,32]{1,0:T(8,128)S(1)}, f32[32,32]{1,0:T(8,128)S(1)}, f32[32,32]{1,0:T(8,128)S(1)}, s32[]{:T(128)}, /*index=5*/s32[]{:T(128)}, ...), condition=%wide.region_25.26_spmd, body=%wide.region_24.25_spmd.sunk | while | flops 12355 | bytes 18937 | solution.py:63
  695.8 45.5 %while.293 = (s32[]{:T(128)}, f32[32,32]{0,1:T(8,128)S(1)}, f32[32,32]{0,1:T(8,128)S(1)}, s32[]{:T(128)}, s32[]{:T(128)}, /*index=5*/s32[]{:T(128)}) while((s32[]{:T(128)}, f32[32,32]{0,1:T(8,128)S(1)}, f32[32,32]{0,1:T(8,128)S(1)}, s32[]{:T(128)}, s32[]{:T(128)}, /*index=5*/s32[]{:T(128)}) %tuple.711), condition=%wide.region_27.28_spmd.clone, body=%wide.region_26.27_spmd.clone.sunk | while | flops 2211 | bytes 10493 | solution.py:48
  741.4 45.1 %while.285 = (s32[]{:T(128)}, f32[32,32]{1,0:T(8,128)S(1)}, f32[32,32]{1,0:T(8,128)S(1)}, f32[32,32]{1,0:T(8,128)S(1)}, s32[]{:T(128)}, /*index=5*/s32[]{:T(128)}, s32[]{:T(128)}) while((s32[]{:T(128)}, f32[32,32]{1,0:T(8,128)S(1)}, f32[32,32]{1,0:T(8,128)S(1)}, f32[32,32]{1,0:T(8,128)S(1)}, s32[]{:T(128)}, /*index=5*/s32[]{:T(128)}, ...), condition=%wide.region_29.30_spmd, body=%wide.region_28.29_spmd.sunk | while | flops 12355 | bytes 18937 | solution.py:63
  787.8 45.5 %while.294 = (s32[]{:T(128)}, f32[32,32]{0,1:T(8,128)S(1)}, f32[32,32]{0,1:T(8,128)S(1)}, s32[]{:T(128)}, s32[]{:T(128)}, /*index=5*/s32[]{:T(128)}) while((s32[]{:T(128)}, f32[32,32]{0,1:T(8,128)S(1)}, f32[32,32]{0,1:T(8,128)S(1)}, s32[]{:T(128)}, s32[]{:T(128)}, /*index=5*/s32[]{:T(128)}) %tuple.717), condition=%wide.region_31.32_spmd.clone, body=%wide.region_30.31_spmd.clone.sunk | while | flops 2211 | bytes 10493 | solution.py:48
  833.4 45.1 %while.286 = (s32[]{:T(128)}, f32[32,32]{1,0:T(8,128)S(1)}, f32[32,32]{1,0:T(8,128)S(1)}, f32[32,32]{1,0:T(8,128)S(1)}, s32[]{:T(128)}, /*index=5*/s32[]{:T(128)}, s32[]{:T(128)}) while((s32[]{:T(128)}, f32[32,32]{1,0:T(8,128)S(1)}, f32[32,32]{1,0:T(8,128)S(1)}, f32[32,32]{1,0:T(8,128)S(1)}, s32[]{:T(128)}, /*index=5*/s32[]{:T(128)}, ...), condition=%wide.region_33.34_spmd, body=%wide.region_32.33_spmd.sunk | while | flops 12355 | bytes 18937 | solution.py:63
  879.0 45.5 %while.295 = (s32[]{:T(128)}, f32[32,32]{0,1:T(8,128)S(1)}, f32[32,32]{0,1:T(8,128)S(1)}, s32[]{:T(128)}, s32[]{:T(128)}, /*index=5*/s32[]{:T(128)}) while((s32[]{:T(128)}, f32[32,32]{0,1:T(8,128)S(1)}, f32[32,32]{0,1:T(8,128)S(1)}, s32[]{:T(128)}, s32[]{:T(128)}, /*index=5*/s32[]{:T(128)}) %tuple.723), condition=%wide.region_35.36_spmd.clone, body=%wide.region_34.35_spmd.clone.sunk | while | flops 2211 | bytes 10493 | solution.py:48
  924.6 45.1 %while.287 = (s32[]{:T(128)}, f32[32,32]{1,0:T(8,128)S(1)}, f32[32,32]{1,0:T(8,128)S(1)}, f32[32,32]{1,0:T(8,128)S(1)}, s32[]{:T(128)}, /*index=5*/s32[]{:T(128)}, s32[]{:T(128)}) while((s32[]{:T(128)}, f32[32,32]{1,0:T(8,128)S(1)}, f32[32,32]{1,0:T(8,128)S(1)}, f32[32,32]{1,0:T(8,128)S(1)}, s32[]{:T(128)}, /*index=5*/s32[]{:T(128)}, ...), condition=%wide.region_37.38_spmd, body=%wide.region_36.37_spmd.sunk | while | flops 12355 | bytes 18937 | solution.py:63
  977.4 0.8 bitcast_reduce_fusion
  985.5 2.8 fusion.48
  (2283 shorter events, 565.0 us)
Async XLA Ops:
  7.2 13.0 %copy-start = (bf16[8,2,256,256]{3,2,1,0:T(8,128)(2,1)S(1)}, bf16[8,2,256,256]{3,2,1,0:T(8,128)(2,1)}, u32[]{:S(2)}) copy-start(bf16[8,2,256,256]{3,2,1,0:T(8,128)(2,1)} %param.37) | copy-start | bytes 6291460
  10.5 16.5 %all-to-all-start.1 = ((f32[32,1,8]{2,1,0:T(1,128)}), f32[32,1,8]{2,1,0:T(1,128)S(1)}, u32[]{:S(2)}, u32[]{:S(2)}) async-start(f32[32,1,8]{2,1,0:T(1,128)} %broadcast_in_dim.126), calls=%async_computation.1 | async-start | bytes 32768 | tf_op jit(solution)/shard_map/all_to_all | solution.py:19
  27.0 34.8 %all-to-all-start = ((bf16[8,2,256,256]{3,1,0,2:T(2,128)(2,1)}), bf16[8,2,256,256]{3,1,0,2:T(2,128)(2,1)}, u32[]{:S(2)}, u32[]{:S(2)}) async-start(bf16[8,2,256,256]{3,1,0,2:T(2,128)(2,1)} %copy.85), calls=%async_computation | async-start | bytes 4194304 | tf_op jit(solution)/shard_map/all_to_all | solution.py:108
  33.4 185.0 %all-reduce.2.cloned.1.call-start = ((), (), s32[]{:S(2)}) async-start(), calls=%async_computation.2 | async-start | bytes 524288 | tf_op jit(solution)/shard_map/psum | solution.py:115
  73.6 3.5 copy-start.1
Sparse Core Ops, SparseCore 0:
  79.3 139.0 all-reduce.1
where the time goes:
time: 1000 us; the launch traced here: 996 us
  local copies, waits for them, and re-layouts  334 us (33%)
  matrix products  242 us (24%)
  loops' own time  186 us (19%)
  waiting for transfers between devices  163 us (16%)
  other arithmetic  32.5 us (3%)
  between operations  21.3 us (2%)
  starting transfers between devices  16 us (2%)
    dot_general x256, matrix products, one_row(): known = jnp.dot(lower_row, inverse, precision=highest)  200 us
    another operation x8, loops' own time, small_factor(): return lax.fori_loop(0, order, one_column, start)[1]  183 us
    dynamic_slice x256, local copies, waits for them, and re-layouts, one_column(): pivot = jnp.sqrt(lax.dynamic_slice_in_dim(column, j, 1)[0])  151 us
    dynamic_slice x256, local copies, waits for them, and re-layouts, one_row(): diag_entry = lax.dynamic_slice_in_dim(lower_row[0], i, 1)[0]  151 us
    psum x1, waiting for transfers between devices, body(): gram = lax.psum(partial_value, ('samp', 'layer'))  135 us
    all_to_all x1, waiting for transfers between devices, body(): lax.all_to_all(jac, 'samp', split_axis=2, concat_axis=0, tiled=True)  27 us
  transfers between devices with their start and end apart: 3, of which 3 were waited for; matrix products, arithmetic and copies ran while one was open for 1% of the time, Pallas kernels for 0%

commit v1 on v0

--- a/solution.py
+++ b/solution.py
@@ -112,7 +112,7 @@
     row_dots = jnp.dot(flat.astype(jnp.float32), col_mean, precision=highest)
     mean_square = jnp.sum(col_mean * col_mean)
     partial_value = (raw_gram - row_dots[:, None] - row_dots[None, :] + mean_square) / total
-    gram = lax.psum(partial_value, ("samp", "layer"))
+    gram = jnp.sum(lax.all_gather(partial_value, ("samp", "layer")), axis=0)
     shift = shift_ratio * jnp.trace(gram) / total
     weights = blocked_solve(gram + shift * jnp.eye(total, dtype=jnp.float32), eps)
     start = lax.axis_index("samp") * s_local

time: 1000 us -> 964 us (0.964)
  waiting for transfers between devices: 163 us -> 94.2 us
  blocking collectives: 0 us -> 37.5 us
  starting transfers between devices: 16 us -> 4 us
    psum x1 -> x0, waiting for transfers between devices: 135 us -> none  [body(): gram = lax.psum(partial_value, ('samp', 'layer'))]
    all_gather x0 -> x1, waiting for transfers between devices: none -> 87.3 us  [body(): gram = jnp.sum(lax.all_gather(partial_value, ('samp', 'layer')), axis=0)]
    all_to_all x0 -> x1, blocking collectives: none -> 37.5 us  [body(): lax.all_to_all(jac, 'samp', split_axis=2, concat_axis=0, tiled=True)]
    all_to_all x1 -> x0, waiting for transfers between devices: 27 us -> none  [body(): lax.all_to_all(jac, 'samp', split_axis=2, concat_axis=0, tiled=True)]
    reduce_sum x0 -> x1, other arithmetic: none -> 12 us  [body(): gram = jnp.sum(lax.all_gather(partial_value, ('samp', 'layer')), axis=0)]
  transfers between devices with their start and end apart: 3 -> 2, of which waited for: 3 -> 2; matrix products, arithmetic and copies ran while one was open for 1% -> 1% of each run, Pallas kernels for 0% -> 0%
where the time goes in v1:
time: 964 us; the launch traced here: 959 us
  local copies, waits for them, and re-layouts  333 us (35%)
  matrix products  242 us (25%)
  loops' own time  187 us (19%)
  waiting for transfers between devices  94.2 us (10%)
  other arithmetic  38.8 us (4%)
  blocking collectives  37.5 us (4%)
  between operations  21.5 us (2%)
    dot_general x256, matrix products, one_row(): known = jnp.dot(lower_row, inverse, precision=highest)  200 us
    another operation x8, loops' own time, small_factor(): return lax.fori_loop(0, order, one_column, start)[1]  184 us
    dynamic_slice x256, local copies, waits for them, and re-layouts, one_column(): pivot = jnp.sqrt(lax.dynamic_slice_in_dim(column, j, 1)[0])  151 us
    dynamic_slice x256, local copies, waits for them, and re-layouts, one_row(): diag_entry = lax.dynamic_slice_in_dim(lower_row[0], i, 1)[0]  151 us
    all_gather x1, waiting for transfers between devices, body(): gram = jnp.sum(lax.all_gather(partial_value, ('samp', 'layer')), axis=0)  87.3 us
    all_to_all x1, blocking collectives, body(): lax.all_to_all(jac, 'samp', split_axis=2, concat_axis=0, tiled=True)  37.5 us
  transfers between devices with their start and end apart: 2, of which 2 were waited for; matrix products, arithmetic and copies ran while one was open for 1% of the time, Pallas kernels for 0%

profile of v1, /device:TPU:1, one launch (start us, length us, event | category | flops | bytes accessed | tf_op | source)
XLA Modules:
  0.0 958.6 jit_solution(615883060011018104)
XLA Ops:
  7.2 1.5 copy-done
  8.8 2.4 convolution_convert_fusion
  11.1 2.2 copy.85
  13.3 37.5 %all_to_all.21 = bf16[8,2,256,256]{3,1,0,2:T(2,128)(2,1)S(1)} all-to-all(bf16[8,2,256,256]{3,1,0,2:T(2,128)(2,1)S(1)} %copy.85), channel_id=1, replica_groups=mesh['samp'=32,'layer'=4] {'samp'}, dimensions={2} | all-to-all | bytes 4194304 | tf_op jit(solution)/shard_map/all_to_all | solution.py:108
  50.8 2.7 copy.136
  53.5 1.2 convert_reduce_fusion
  54.7 4.2 reshape.493
  59.6 3.5 fusion.238
  63.1 2.1 fusion.52
  66.4 4.0 all-to-all-start.1
  70.3 6.8 all-to-all-done.1
  79.2 3.6 copy.129
  82.8 87.3 %all-gather.3.cloned.1.call-done = f32[32768,256]{1,0:T(8,128)} async-done(((f32[256,256]{1,0:T(8,128)}), f32[32768,256]{1,0:T(8,128)}) %all-gather.3.cloned.1.call-update) | async-done | bytes 33554448 | tf_op jit(solution)/shard_map/all_gather | solution.py:115
  170.1 12.0 %reduce_sum.98 = f32[256,256]{1,0:T(8,128)S(1)} reduce(f32[128,256,256]{2,1,0:T(8,128)} %bitcast.1120, f32[]{:T(128)} %constant.1438.clone.1), dimensions={0}, to_apply=%region_2.3 | reduce | flops 8323072 | bytes 33816580 | tf_op jit(solution)/shard_map/reduce_sum | solution.py:115
  183.5 45.5 %while.288 = (s32[]{:T(128)}, f32[32,32]{0,1:T(8,128)S(1)}, f32[32,32]{0,1:T(8,128)S(1)}, s32[]{:T(128)}, s32[]{:T(128)}, /*index=5*/s32[]{:T(128)}) while((s32[]{:T(128)}, f32[32,32]{0,1:T(8,128)S(1)}, f32[32,32]{0,1:T(8,128)S(1)}, s32[]{:T(128)}, s32[]{:T(128)}, /*index=5*/s32[]{:T(128)}) %tuple.681), condition=%wide.region_5.6_spmd.clone, body=%wide.region_4.5_spmd.clone.sunk | while | flops 2211 | bytes 10993 | solution.py:48
  229.1 45.1 %while.280 = (s32[]{:T(128)}, f32[32,32]{1,0:T(8,128)S(1)}, f32[32,32]{1,0:T(8,128)S(1)}, f32[32,32]{1,0:T(8,128)S(1)}, s32[]{:T(128)}, /*index=5*/s32[]{:T(128)}, s32[]{:T(128)}) while((s32[]{:T(128)}, f32[32,32]{1,0:T(8,128)S(1)}, f32[32,32]{1,0:T(8,128)S(1)}, f32[32,32]{1,0:T(8,128)S(1)}, s32[]{:T(128)}, /*index=5*/s32[]{:T(128)}, ...), condition=%wide.region_7.8_spmd, body=%wide.region_6.7_spmd.sunk | while | flops 12355 | bytes 19437 | solution.py:63
  231.1 0.8 fusion.577
  232.5 0.8 fusion.577
  235.3 0.8 fusion.577
  238.2 0.8 fusion.577
  239.6 0.8 fusion.577
  242.4 0.8 fusion.577
  243.8 0.8 fusion.577
  246.6 0.8 fusion.577
  248.0 0.8 fusion.577
  249.4 0.8 fusion.577
  250.8 0.8 fusion.577
  253.7 0.8 fusion.577
  255.1 0.8 fusion.577
  257.9 0.8 fusion.577
  259.3 0.8 fusion.577
  279.9 45.6 %while.289 = (s32[]{:T(128)}, f32[32,32]{0,1:T(8,128)S(1)}, f32[32,32]{0,1:T(8,128)S(1)}, s32[]{:T(128)}, s32[]{:T(128)}, /*index=5*/s32[]{:T(128)}) while((s32[]{:T(128)}, f32[32,32]{0,1:T(8,128)S(1)}, f32[32,32]{0,1:T(8,128)S(1)}, s32[]{:T(128)}, s32[]{:T(128)}, /*index=5*/s32[]{:T(128)}) %tuple.687), condition=%wide.region_11.12_spmd.clone, body=%wide.region_10.11_spmd.clone.sunk | while | flops 2211 | bytes 10993 | solution.py:48
  325.5 45.1 %while.281 = (s32[]{:T(128)}, f32[32,32]{1,0:T(8,128)S(1)}, f32[32,32]{1,0:T(8,128)S(1)}, f32[32,32]{1,0:T(8,128)S(1)}, s32[]{:T(128)}, /*index=5*/s32[]{:T(128)}, s32[]{:T(128)}) while((s32[]{:T(128)}, f32[32,32]{1,0:T(8,128)S(1)}, f32[32,32]{1,0:T(8,128)S(1)}, f32[32,32]{1,0:T(8,128)S(1)}, s32[]{:T(128)}, /*index=5*/s32[]{:T(128)}, ...), condition=%wide.region_13.14_spmd, body=%wide.region_12.13_spmd.sunk | while | flops 12355 | bytes 19437 | solution.py:63
  371.8 45.5 %while.290 = (s32[]{:T(128)}, f32[32,32]{0,1:T(8,128)S(1)}, f32[32,32]{0,1:T(8,128)S(1)}, s32[]{:T(128)}, s32[]{:T(128)}, /*index=5*/s32[]{:T(128)}) while((s32[]{:T(128)}, f32[32,32]{0,1:T(8,128)S(1)}, f32[32,32]{0,1:T(8,128)S(1)}, s32[]{:T(128)}, s32[]{:T(128)}, /*index=5*/s32[]{:T(128)}) %tuple.693), condition=%wide.region_15.16_spmd.clone, body=%wide.region_14.15_spmd.clone.sunk | while | flops 2211 | bytes 10993 | solution.py:48
  417.4 45.1 %while.282 = (s32[]{:T(128)}, f32[32,32]{1,0:T(8,128)S(1)}, f32[32,32]{1,0:T(8,128)S(1)}, f32[32,32]{1,0:T(8,128)S(1)}, s32[]{:T(128)}, /*index=5*/s32[]{:T(128)}, s32[]{:T(128)}) while((s32[]{:T(128)}, f32[32,32]{1,0:T(8,128)S(1)}, f32[32,32]{1,0:T(8,128)S(1)}, f32[32,32]{1,0:T(8,128)S(1)}, s32[]{:T(128)}, /*index=5*/s32[]{:T(128)}, ...), condition=%wide.region_17.18_spmd, body=%wide.region_16.17_spmd.sunk | while | flops 12355 | bytes 19437 | solution.py:63
  464.4 45.5 %while.291 = (s32[]{:T(128)}, f32[32,32]{0,1:T(8,128)S(1)}, f32[32,32]{0,1:T(8,128)S(1)}, s32[]{:T(128)}, s32[]{:T(128)}, /*index=5*/s32[]{:T(128)}) while((s32[]{:T(128)}, f32[32,32]{0,1:T(8,128)S(1)}, f32[32,32]{0,1:T(8,128)S(1)}, s32[]{:T(128)}, s32[]{:T(128)}, /*index=5*/s32[]{:T(128)}) %tuple.699), condition=%wide.region_19.20_spmd.clone, body=%wide.region_18.19_spmd.clone.sunk | while | flops 2211 | bytes 10993 | solution.py:48
  510.0 45.1 %while.283 = (s32[]{:T(128)}, f32[32,32]{1,0:T(8,128)S(1)}, f32[32,32]{1,0:T(8,128)S(1)}, f32[32,32]{1,0:T(8,128)S(1)}, s32[]{:T(128)}, /*index=5*/s32[]{:T(128)}, s32[]{:T(128)}) while((s32[]{:T(128)}, f32[32,32]{1,0:T(8,128)S(1)}, f32[32,32]{1,0:T(8,128)S(1)}, f32[32,32]{1,0:T(8,128)S(1)}, s32[]{:T(128)}, /*index=5*/s32[]{:T(128)}, ...), condition=%wide.region_21.22_spmd, body=%wide.region_20.21_spmd.sunk | while | flops 12355 | bytes 19437 | solution.py:63
  557.9 45.5 %while.292 = (s32[]{:T(128)}, f32[32,32]{0,1:T(8,128)S(1)}, f32[32,32]{0,1:T(8,128)S(1)}, s32[]{:T(128)}, s32[]{:T(128)}, /*index=5*/s32[]{:T(128)}) while((s32[]{:T(128)}, f32[32,32]{0,1:T(8,128)S(1)}, f32[32,32]{0,1:T(8,128)S(1)}, s32[]{:T(128)}, s32[]{:T(128)}, /*index=5*/s32[]{:T(128)}) %tuple.705), condition=%wide.region_23.24_spmd.clone, body=%wide.region_22.23_spmd.clone.sunk | while | flops 2211 | bytes 10993 | solution.py:48
  603.5 45.1 %while.284 = (s32[]{:T(128)}, f32[32,32]{1,0:T(8,128)S(1)}, f32[32,32]{1,0:T(8,128)S(1)}, f32[32,32]{1,0:T(8,128)S(1)}, s32[]{:T(128)}, /*index=5*/s32[]{:T(128)}, s32[]{:T(128)}) while((s32[]{:T(128)}, f32[32,32]{1,0:T(8,128)S(1)}, f32[32,32]{1,0:T(8,128)S(1)}, f32[32,32]{1,0:T(8,128)S(1)}, s32[]{:T(128)}, /*index=5*/s32[]{:T(128)}, ...), condition=%wide.region_25.26_spmd, body=%wide.region_24.25_spmd.sunk | while | flops 12355 | bytes 19437 | solution.py:63
  652.6 45.5 %while.293 = (s32[]{:T(128)}, f32[32,32]{0,1:T(8,128)S(1)}, f32[32,32]{0,1:T(8,128)S(1)}, s32[]{:T(128)}, s32[]{:T(128)}, /*index=5*/s32[]{:T(128)}) while((s32[]{:T(128)}, f32[32,32]{0,1:T(8,128)S(1)}, f32[32,32]{0,1:T(8,128)S(1)}, s32[]{:T(128)}, s32[]{:T(128)}, /*index=5*/s32[]{:T(128)}) %tuple.711), condition=%wide.region_27.28_spmd.clone, body=%wide.region_26.27_spmd.clone.sunk | while | flops 2211 | bytes 10993 | solution.py:48
  698.2 45.1 %while.285 = (s32[]{:T(128)}, f32[32,32]{1,0:T(8,128)S(1)}, f32[32,32]{1,0:T(8,128)S(1)}, f32[32,32]{1,0:T(8,128)S(1)}, s32[]{:T(128)}, /*index=5*/s32[]{:T(128)}, s32[]{:T(128)}) while((s32[]{:T(128)}, f32[32,32]{1,0:T(8,128)S(1)}, f32[32,32]{1,0:T(8,128)S(1)}, f32[32,32]{1,0:T(8,128)S(1)}, s32[]{:T(128)}, /*index=5*/s32[]{:T(128)}, ...), condition=%wide.region_29.30_spmd, body=%wide.region_28.29_spmd.sunk | while | flops 12355 | bytes 19437 | solution.py:63
  745.4 45.5 %while.294 = (s32[]{:T(128)}, f32[32,32]{0,1:T(8,128)S(1)}, f32[32,32]{0,1:T(8,128)S(1)}, s32[]{:T(128)}, s32[]{:T(128)}, /*index=5*/s32[]{:T(128)}) while((s32[]{:T(128)}, f32[32,32]{0,1:T(8,128)S(1)}, f32[32,32]{0,1:T(8,128)S(1)}, s32[]{:T(128)}, s32[]{:T(128)}, /*index=5*/s32[]{:T(128)}) %tuple.717), condition=%wide.region_31.32_spmd.clone, body=%wide.region_30.31_spmd.clone.sunk | while | flops 2211 | bytes 10993 | solution.py:48
  791.0 45.1 %while.286 = (s32[]{:T(128)}, f32[32,32]{1,0:T(8,128)S(1)}, f32[32,32]{1,0:T(8,128)S(1)}, f32[32,32]{1,0:T(8,128)S(1)}, s32[]{:T(128)}, /*index=5*/s32[]{:T(128)}, s32[]{:T(128)}) while((s32[]{:T(128)}, f32[32,32]{1,0:T(8,128)S(1)}, f32[32,32]{1,0:T(8,128)S(1)}, f32[32,32]{1,0:T(8,128)S(1)}, s32[]{:T(128)}, /*index=5*/s32[]{:T(128)}, ...), condition=%wide.region_33.34_spmd, body=%wide.region_32.33_spmd.sunk | while | flops 12355 | bytes 19437 | solution.py:63
  841.6 45.6 %while.295 = (s32[]{:T(128)}, f32[32,32]{0,1:T(8,128)S(1)}, f32[32,32]{0,1:T(8,128)S(1)}, s32[]{:T(128)}, s32[]{:T(128)}, /*index=5*/s32[]{:T(128)}) while((s32[]{:T(128)}, f32[32,32]{0,1:T(8,128)S(1)}, f32[32,32]{0,1:T(8,128)S(1)}, s32[]{:T(128)}, s32[]{:T(128)}, /*index=5*/s32[]{:T(128)}) %tuple.723), condition=%wide.region_35.36_spmd.clone, body=%wide.region_34.35_spmd.clone.sunk | while | flops 2211 | bytes 10993 | solution.py:48
  887.2 45.1 %while.287 = (s32[]{:T(128)}, f32[32,32]{1,0:T(8,128)S(1)}, f32[32,32]{1,0:T(8,128)S(1)}, f32[32,32]{1,0:T(8,128)S(1)}, s32[]{:T(128)}, /*index=5*/s32[]{:T(128)}, s32[]{:T(128)}) while((s32[]{:T(128)}, f32[32,32]{1,0:T(8,128)S(1)}, f32[32,32]{1,0:T(8,128)S(1)}, f32[32,32]{1,0:T(8,128)S(1)}, s32[]{:T(128)}, /*index=5*/s32[]{:T(128)}, ...), condition=%wide.region_37.38_spmd, body=%wide.region_36.37_spmd.sunk | while | flops 12355 | bytes 19437 | solution.py:63
  934.5 0.8 bitcast_reduce_fusion.4
  938.5 0.8 bitcast_reduce_fusion.1
  947.8 2.8 fusion.48
  (2287 shorter events, 562.6 us)
Async XLA Ops:
  7.2 1.6 copy-start
  7.2 162.9 %all-gather.3.cloned.1.call-start = ((), (), s32[]{:S(2)}) async-start(), calls=%async_computation.2 | async-start | bytes 33816576 | tf_op jit(solution)/shard_map/all_gather | solution.py:115
  59.6 3.5 copy-start.1
  63.0 2.2 copy-start.2
  63.1 2.7 copy-start.3
  66.4 10.8 %all-to-all-start.1 = ((f32[32,1,8]{2,1,0:T(1,128)}), f32[32,1,8]{2,1,0:T(1,128)S(1)}, u32[]{:S(2)}, u32[]{:S(2)}) async-start(f32[32,1,8]{2,1,0:T(1,128)} %broadcast_in_dim.126), calls=%async_computation.1 | async-start | bytes 32768 | tf_op jit(solution)/shard_map/all_to_all | solution.py:19
Sparse Core Ops, SparseCore 0:
  65.3 104.7 all-gather.2
